TPU v7x, 32 devices: a whole 2x2x4 slice. The times are simulated.
32 devices in a mesh: fsdp: 8 (over z, x), tp: 4 (over y, core).
Axes of the slice: x: 2, y: 2, z: 4, core: 2. Of those that a mesh axis runs over, the one named last changes fastest.
Arguments:
- tokens: bfloat16 [8, 2048, 768], P('fsdp', 'tp'), may hold values from -6 to 6
- lengths: int32 [8, 4], P('fsdp'), may hold values from 288 to 1024, as said below
- pictures: int32 [8, 2048], P('fsdp'), may hold values from 0 to 3, as said below
- w_query: bfloat16 [768, 768], P('fsdp', 'tp'), may hold values from -0.21875 to 0.21875
- w_key: bfloat16 [768, 768], P('fsdp', 'tp'), may hold values from -0.21875 to 0.21875
- w_value: bfloat16 [768, 768], P('fsdp', 'tp'), may hold values from -0.21875 to 0.21875
- w_out: bfloat16 [768, 768], P('tp', 'fsdp'), may hold values from -0.875 to 0.875
- w_up: bfloat16 [768, 3072], P('fsdp', 'tp'), may hold values from -0.21875 to 0.21875
- w_down: bfloat16 [3072, 768], P('tp', 'fsdp'), may hold values from -0.15625 to 0.15625
- norm1_gain: float32 [768], P(('fsdp', 'tp')), may hold values from 0.5 to 1.5
- norm1_shift: float32 [768], P(('fsdp', 'tp')), may hold values from -1.75 to 1.75
- norm2_gain: float32 [768], P(('fsdp', 'tp')), may hold values from 0.5 to 1.5
- norm2_shift: float32 [768], P(('fsdp', 'tp')), may hold values from -1.75 to 1.75
- query_gain: float32 [768], P(('fsdp', 'tp')), may hold values from 1 to 2
- key_gain: float32 [768], P(('fsdp', 'tp')), may hold values from 1 to 2
- cotangent: bfloat16 [8, 2048, 768], P('fsdp', 'tp'), may hold values from -6 to 6
Outputs:
- layer_out: bfloat16 [8, 2048, 768], P('fsdp', 'tp')
- input_grad: float32 [8, 2048, 768], P('fsdp', 'tp')
- grad_query: float32 [768, 768], P('fsdp', 'tp')
- grad_key: float32 [768, 768], P('fsdp', 'tp')
- grad_value: float32 [768, 768], P('fsdp', 'tp')
- grad_output_proj: float32 [768, 768], P('tp', 'fsdp')
- grad_up: float32 [768, 3072], P('fsdp', 'tp')
- grad_down: float32 [3072, 768], P('tp', 'fsdp')
- grad_norm1_gain: float32 [768], P(('fsdp', 'tp'))
- grad_norm1_shift: float32 [768], P(('fsdp', 'tp'))
- grad_norm2_gain: float32 [768], P(('fsdp', 'tp'))
- grad_norm2_shift: float32 [768], P(('fsdp', 'tp'))
- grad_query_gain: float32 [768], P(('fsdp', 'tp'))
- grad_key_gain: float32 [768], P(('fsdp', 'tp'))
- statistics: float32 [4], replicated
Inputs may be any that keep to these rules, and one draw needn't show every extreme that they name: The lengths of a row sum to at most 2048; one picture of every row has exactly 1024 patches. Slots of a row carry the pictures in order, each picture covering as many slots as its length; slots after the row's total length repeat the last picture's number.
All inputs are finite; a program needn't handle non-finite values.
Results may differ from a plain program's by a relative error of at most 0.018.
Values may be sent and summed in bfloat16 or wider, within the bound.
A program may use at most 192 MiB of HBM per device.

v0:
```python
import jax
import jax.numpy as jnp
from jax import lax
from jax.sharding import PartitionSpec as P

HD = 64
EPS = 1e-06
ROOT_HALF = 0.7071067811865476
DENSITY = 0.3989422804014327


def normalise(values, scaling, offset):
    centre = jnp.mean(values, axis=-1, keepdims=True)
    centred = values - centre
    spread = jnp.mean(centred * centred, axis=-1, keepdims=True)
    inverse = lax.rsqrt(spread + EPS)
    normed = centred * inverse
    return (normed * scaling + offset, normed, inverse)


def normalise_back(grad_out, normed, inverse, scaling):
    grad_unit = grad_out * scaling
    grad_values = inverse * (
        grad_unit
        - jnp.mean(grad_unit, axis=-1, keepdims=True)
        - normed * jnp.mean(grad_unit * normed, axis=-1, keepdims=True)
    )
    return (grad_values, jnp.sum(grad_out * normed, axis=(0, 1)), jnp.sum(grad_out, axis=(0, 1)))


def gelu_slope(values):
    return (
        0.5 * (1.0 + jax.scipy.special.erf(values * ROOT_HALF))
        + values * jnp.exp(-0.5 * values * values) * DENSITY
    )


def gather_tokens(values):
    return lax.all_gather(values, "tp", axis=1, tiled=True)


def gather_grads(values):
    return lax.all_gather(values, "tp", axis=1, tiled=True)


def reduce_tokens(values):
    return lax.psum_scatter(
        values.astype(jnp.bfloat16), "tp", scatter_dimension=1, tiled=True
    ).astype(jnp.float32)


def reduce_grads(values):
    return lax.psum_scatter(
        values.astype(jnp.bfloat16), "tp", scatter_dimension=1, tiled=True
    ).astype(jnp.float32)


def block_scores(query, keyed, picture_query, picture_key, key_mask):
    raw_scores = jnp.einsum("qhd,khd->hqk", query, keyed, preferred_element_type=jnp.float32)
    allowed = (picture_query[:, None] == picture_key[None, :]) & (key_mask[None, :] > 0)
    return jnp.where(allowed[None], raw_scores * query.shape[-1] ** (-0.5), -1e30)


def forward_row(packed):
    query_row, key_row, value_row, picture_row, mask_row = packed
    full_len = query_row.shape[0]
    block_len = min(512, full_len)
    block_count = full_len // block_len

    def forward_one_block(packed_block):
        query_block, picture_block = packed_block
        scores = block_scores(query_block, key_row, picture_block, picture_row, mask_row)
        highest = jnp.max(scores, axis=-1, keepdims=True)
        logsum = highest + jnp.log(jnp.sum(jnp.exp(scores - highest), axis=-1, keepdims=True))
        probability = jnp.exp(scores - logsum).astype(jnp.bfloat16)
        mixture = jnp.einsum(
            "hqk,khd->qhd", probability, value_row, preferred_element_type=jnp.float32
        )
        return (mixture, logsum)

    query_blocks = query_row.reshape((block_count, block_len) + query_row.shape[1:])
    return lax.map(forward_one_block, (query_blocks, picture_row.reshape(block_count, block_len)))


def backward_row(packed):
    query_row, key_row, value_row, picture_row, mask_row, grad_row, logsum_row = packed
    full_len = query_row.shape[0]
    block_len = min(512, full_len)
    block_count = full_len // block_len
    factor = query_row.shape[-1] ** (-0.5)

    def backward_one_block(running, packed_block):
        grad_key, grad_value = running
        query_block, picture_block, grad_block, logsum_block = packed_block
        scores = block_scores(query_block, key_row, picture_block, picture_row, mask_row)
        probability = jnp.exp(scores - logsum_block)
        prob_low = probability.astype(jnp.bfloat16)
        grad_prob = jnp.einsum(
            "qhd,khd->hqk", grad_block, value_row, preferred_element_type=jnp.float32
        )
        grad_value = grad_value + jnp.einsum(
            "hqk,qhd->khd", prob_low, grad_block, preferred_element_type=jnp.float32
        )
        centre = jnp.sum(probability * grad_prob, axis=-1, keepdims=True)
        grad_scores = (probability * (grad_prob - centre)).astype(jnp.bfloat16)
        grad_query = factor * jnp.einsum(
            "hqk,khd->qhd", grad_scores, key_row, preferred_element_type=jnp.float32
        )
        grad_key = grad_key + factor * jnp.einsum(
            "hqk,qhd->khd", grad_scores, query_block, preferred_element_type=jnp.float32
        )
        return ((grad_key, grad_value), grad_query)

    zero_state = jnp.zeros(key_row.shape, jnp.float32)
    block_shape = (block_count, block_len) + query_row.shape[1:]
    (grad_key, grad_value), grad_query = lax.scan(
        backward_one_block,
        (zero_state, zero_state),
        (
            query_row.reshape(block_shape),
            picture_row.reshape(block_count, block_len),
            grad_row.reshape(block_shape),
            logsum_row,
        ),
    )
    return (grad_query.reshape(key_row.shape), grad_key, grad_value)


def local(
    tokens,
    lengths,
    pictures,
    w_query,
    w_key,
    w_value,
    w_out,
    w_up,
    w_down,
    norm1_gain,
    norm1_shift,
    norm2_gain,
    norm2_shift,
    query_gain,
    key_gain,
    cotangent,
):
    tp_place = lax.axis_index("tp")
    local_len = tokens.shape[1]
    model_width = tokens.shape[2]
    full_len = pictures.shape[1]
    local_width = w_query.shape[1]
    heads_local = local_width // HD
    gain_one, shift_one, gain_two, shift_two, gain_query, gain_key = (
        lax.all_gather(norm1_gain, ("fsdp", "tp"), axis=0, tiled=True),
        lax.all_gather(norm1_shift, ("fsdp", "tp"), axis=0, tiled=True),
        lax.all_gather(norm2_gain, ("fsdp", "tp"), axis=0, tiled=True),
        lax.all_gather(norm2_shift, ("fsdp", "tp"), axis=0, tiled=True),
        lax.all_gather(query_gain, ("fsdp", "tp"), axis=0, tiled=True),
        lax.all_gather(key_gain, ("fsdp", "tp"), axis=0, tiled=True),
    )
    positions = jnp.arange(full_len, dtype=jnp.int32)
    valid_full = (positions[None, :] < jnp.sum(lengths, axis=1)[:, None]).astype(jnp.float32)
    valid_here = lax.dynamic_slice_in_dim(valid_full, tp_place * local_len, local_len, 1)[
        :, :, None
    ]
    qgain_here = lax.dynamic_slice_in_dim(
        gain_query, tp_place * local_width, local_width, 0
    ).reshape(heads_local, HD)
    kgain_here = lax.dynamic_slice_in_dim(gain_key, tp_place * local_width, local_width, 0).reshape(
        heads_local, HD
    )
    front_query, front_key, front_value, front_out = (
        lax.all_gather(w_query, "fsdp", axis=0, tiled=True),
        lax.all_gather(w_key, "fsdp", axis=0, tiled=True),
        lax.all_gather(w_value, "fsdp", axis=0, tiled=True),
        lax.all_gather(w_out, "fsdp", axis=1, tiled=True),
    )
    inputs = tokens.astype(jnp.float32)
    hidden, normed_one, inverse_one = normalise(inputs, gain_one, shift_one)
    hidden_full = gather_tokens(hidden.astype(jnp.bfloat16))
    row_shape = hidden_full.shape[:2] + (heads_local, HD)
    query = jnp.dot(hidden_full, front_query, preferred_element_type=jnp.float32).reshape(row_shape)
    keyed = jnp.dot(hidden_full, front_key, preferred_element_type=jnp.float32).reshape(row_shape)
    value_low = (
        jnp.dot(hidden_full, front_value, preferred_element_type=jnp.float32)
        .astype(jnp.bfloat16)
        .reshape(row_shape)
    )
    query_norm, query_unit, query_inverse = normalise(query, qgain_here, 0.0)
    key_norm, key_unit, key_inverse = normalise(keyed, kgain_here, 0.0)
    query_low = query_norm.astype(jnp.bfloat16)
    key_low = key_norm.astype(jnp.bfloat16)
    mixture, logsum = lax.map(forward_row, (query_low, key_low, value_low, pictures, valid_full))
    mixture_low = mixture.reshape(hidden_full.shape[:2] + (local_width,)).astype(jnp.bfloat16)
    attn_branch = valid_here * reduce_tokens(
        jnp.dot(mixture_low, front_out, preferred_element_type=jnp.float32)
    )
    middle = inputs + attn_branch
    hidden_two, normed_two, inverse_two = normalise(middle, gain_two, shift_two)
    hidden_two_full = gather_tokens(hidden_two.astype(jnp.bfloat16))
    front_up, front_down = (
        lax.all_gather(w_up, "fsdp", axis=0, tiled=True),
        lax.all_gather(w_down, "fsdp", axis=1, tiled=True),
    )
    up_value = jnp.dot(hidden_two_full, front_up, preferred_element_type=jnp.float32)
    activated = jax.nn.gelu(up_value, approximate=False).astype(jnp.bfloat16)
    mlp_branch = valid_here * reduce_tokens(
        jnp.dot(activated, front_down, preferred_element_type=jnp.float32)
    )
    result = (middle + mlp_branch).astype(jnp.bfloat16)
    square_sums = jnp.stack(
        [
            jnp.sum(valid_here * inputs * inputs),
            jnp.sum(attn_branch * attn_branch),
            jnp.sum(valid_here * middle * middle),
            jnp.sum(mlp_branch * mlp_branch),
        ]
    )
    valid_count = jnp.sum(valid_here)
    back_up, back_down = (
        lax.all_gather(w_up, "fsdp", axis=0, tiled=True),
        lax.all_gather(w_down, "fsdp", axis=1, tiled=True),
    )
    back_query, back_key, back_value, back_out = (
        lax.all_gather(w_query, "fsdp", axis=0, tiled=True),
        lax.all_gather(w_key, "fsdp", axis=0, tiled=True),
        lax.all_gather(w_value, "fsdp", axis=0, tiled=True),
        lax.all_gather(w_out, "fsdp", axis=1, tiled=True),
    )
    grad_y = cotangent.astype(jnp.float32) * valid_here
    grad_y_full = gather_grads(grad_y.astype(jnp.bfloat16))
    grad_down = jnp.einsum(
        "rlf,rld->fd", activated, grad_y_full, preferred_element_type=jnp.float32
    )
    grad_act = jnp.dot(grad_y_full, back_down.T, preferred_element_type=jnp.float32)
    grad_pre = (grad_act * gelu_slope(up_value)).astype(jnp.bfloat16)
    grad_up = jnp.einsum(
        "rld,rlf->df", hidden_two_full, grad_pre, preferred_element_type=jnp.float32
    )
    grad_hidden_two = reduce_grads(jnp.dot(grad_pre, back_up.T, preferred_element_type=jnp.float32))
    mlp_grads = (
        lax.psum_scatter(grad_up, "fsdp", scatter_dimension=0, tiled=True),
        lax.psum_scatter(grad_down, "fsdp", scatter_dimension=1, tiled=True),
    )
    grad_mid_norm, grad_gain_two, grad_shift_two = normalise_back(
        grad_hidden_two, normed_two, inverse_two, gain_two
    )
    grad_middle = grad_y + grad_mid_norm
    grad_branch_here = (valid_here * grad_middle).astype(jnp.bfloat16)
    grad_branch_full = gather_grads(grad_branch_here)
    grad_out_proj = jnp.einsum(
        "rlh,rld->hd", mixture_low, grad_branch_full, preferred_element_type=jnp.float32
    )
    grad_mixture = jnp.dot(grad_branch_full, back_out.T, preferred_element_type=jnp.float32).astype(
        jnp.bfloat16
    )
    grad_qnorm, grad_knorm, grad_value_full = lax.map(
        backward_row,
        (
            query_low,
            key_low,
            value_low,
            pictures,
            valid_full,
            grad_mixture.reshape(row_shape),
            logsum,
        ),
    )
    grad_query_pre, grad_qgain, unused_one = normalise_back(
        grad_qnorm, query_unit, query_inverse, qgain_here
    )
    grad_key_pre, grad_kgain, unused_two = normalise_back(
        grad_knorm, key_unit, key_inverse, kgain_here
    )
    flat_shape = hidden_full.shape[:2] + (local_width,)
    grad_query_low = grad_query_pre.reshape(flat_shape).astype(jnp.bfloat16)
    grad_key_low = grad_key_pre.reshape(flat_shape).astype(jnp.bfloat16)
    grad_value_low = grad_value_full.reshape(flat_shape).astype(jnp.bfloat16)
    grad_wquery = jnp.einsum(
        "rld,rlh->dh", hidden_full, grad_query_low, preferred_element_type=jnp.float32
    )
    grad_wkey = jnp.einsum(
        "rld,rlh->dh", hidden_full, grad_key_low, preferred_element_type=jnp.float32
    )
    grad_wvalue = jnp.einsum(
        "rld,rlh->dh", hidden_full, grad_value_low, preferred_element_type=jnp.float32
    )
    grad_hidden_part = (
        jnp.dot(grad_query_low, back_query.T, preferred_element_type=jnp.float32)
        + jnp.dot(grad_key_low, back_key.T, preferred_element_type=jnp.float32)
        + jnp.dot(grad_value_low, back_value.T, preferred_element_type=jnp.float32)
    )
    grad_hidden = reduce_grads(grad_hidden_part)
    attn_grads = (
        lax.psum_scatter(grad_wquery, "fsdp", scatter_dimension=0, tiled=True),
        lax.psum_scatter(grad_wkey, "fsdp", scatter_dimension=0, tiled=True),
        lax.psum_scatter(grad_wvalue, "fsdp", scatter_dimension=0, tiled=True),
        lax.psum_scatter(grad_out_proj, "fsdp", scatter_dimension=1, tiled=True),
    )
    grad_in_norm, grad_gain_one, grad_shift_one = normalise_back(
        grad_hidden, normed_one, inverse_one, gain_one
    )
    grad_inputs = grad_middle + grad_in_norm
    zero_width = jnp.zeros((model_width,), jnp.float32)
    grad_qgain_full = lax.dynamic_update_slice_in_dim(
        zero_width, grad_qgain.reshape(local_width), tp_place * local_width, 0
    )
    grad_kgain_full = lax.dynamic_update_slice_in_dim(
        zero_width, grad_kgain.reshape(local_width), tp_place * local_width, 0
    )
    small_shards = (
        lax.psum_scatter(grad_gain_one, ("fsdp", "tp"), scatter_dimension=0, tiled=True),
        lax.psum_scatter(grad_shift_one, ("fsdp", "tp"), scatter_dimension=0, tiled=True),
        lax.psum_scatter(grad_gain_two, ("fsdp", "tp"), scatter_dimension=0, tiled=True),
        lax.psum_scatter(grad_shift_two, ("fsdp", "tp"), scatter_dimension=0, tiled=True),
        lax.psum_scatter(grad_qgain_full, ("fsdp", "tp"), scatter_dimension=0, tiled=True),
        lax.psum_scatter(grad_kgain_full, ("fsdp", "tp"), scatter_dimension=0, tiled=True),
    )
    totals, counted = lax.psum((square_sums, valid_count), ("fsdp", "tp"))
    statistics = jnp.sqrt(totals / (counted * model_width))
    return (
        result,
        grad_inputs,
        attn_grads[0],
        attn_grads[1],
        attn_grads[2],
        attn_grads[3],
        mlp_grads[0],
        mlp_grads[1],
        small_shards[0],
        small_shards[1],
        small_shards[2],
        small_shards[3],
        small_shards[4],
        small_shards[5],
        statistics,
    )


def solution(mesh):
    in_specs = (
        P("fsdp", "tp", None),
        P("fsdp", None),
        P("fsdp", None),
        P("fsdp", "tp"),
        P("fsdp", "tp"),
        P("fsdp", "tp"),
        P("tp", "fsdp"),
        P("fsdp", "tp"),
        P("tp", "fsdp"),
        P(("fsdp", "tp")),
        P(("fsdp", "tp")),
        P(("fsdp", "tp")),
        P(("fsdp", "tp")),
        P(("fsdp", "tp")),
        P(("fsdp", "tp")),
        P("fsdp", "tp", None),
    )
    out_specs = (
        P("fsdp", "tp", None),
        P("fsdp", "tp", None),
        P("fsdp", "tp"),
        P("fsdp", "tp"),
        P("fsdp", "tp"),
        P("tp", "fsdp"),
        P("fsdp", "tp"),
        P("tp", "fsdp"),
        P(("fsdp", "tp")),
        P(("fsdp", "tp")),
        P(("fsdp", "tp")),
        P(("fsdp", "tp")),
        P(("fsdp", "tp")),
        P(("fsdp", "tp")),
        P(),
    )
    return jax.shard_map(local, mesh=mesh, in_specs=in_specs, out_specs=out_specs, check_vma=False)
```

profile of v0, /device:TPU:0, one launch (start us, length us, event | category | flops | bytes accessed | tf_op | source)
XLA Modules:
  0.0 1174.1 jit_solution(14461486698308457316)
XLA Ops:
  16.0 42.4 %all-reduce.13 = (f32[768]{0:T(1024)}, f32[768]{0:T(1024)}, f32[768]{0:T(1024)S(1)}, f32[768]{0:T(1024)S(1)}, f32[768]{0:T(1024)S(1)}, /*index=5*/f32[768]{0:T(1024)S(1)}) all-reduce(f32[768]{0:T(1024)S(1)} %dynamic-update-slice.5, f32[768]{0:T(1024)S(1)} %dynamic-update-slice.4, ...), channel_id=1, replica_groups=mesh['fsdp'=8,'tp'=4] {'fsdp','tp'}, use_global_device_ids=true, to_apply=%add.5 | all-reduce | flops 4608 | bytes 36864
  63.4 31.0 %all_gather.62 = bf16[192,768]{0,1:T(8,128)(2,1)S(1)} all-gather(bf16[192,96]{0,1:T(8,128)(2,1)S(1)} %copy.45), channel_id=1, replica_groups=mesh['fsdp'=8,'tp'=4] {'fsdp'}, dimensions={1}, use_global_device_ids=true | all-gather | bytes 331776 | tf_op jit(solution)/shard_map/all_gather | solution.py:176
  94.4 31.2 %all_gather.57 = bf16[768,192]{1,0:T(8,128)(2,1)S(1)} all-gather(bf16[96,192]{1,0:T(8,128)(2,1)S(1)} %copy-done.54), channel_id=1, replica_groups=mesh['fsdp'=8,'tp'=4] {'fsdp'}, dimensions={0}, use_global_device_ids=true | all-gather | bytes 331776 | tf_op jit(solution)/shard_map/all_gather | solution.py:173
  125.7 31.1 %all_gather.59 = bf16[768,192]{1,0:T(8,128)(2,1)S(1)} all-gather(bf16[96,192]{1,0:T(8,128)(2,1)S(1)} %copy-done.55), channel_id=1, replica_groups=mesh['fsdp'=8,'tp'=4] {'fsdp'}, dimensions={0}, use_global_device_ids=true | all-gather | bytes 331776 | tf_op jit(solution)/shard_map/all_gather | solution.py:174
  156.8 33.0 %all_gather.61 = bf16[768,192]{1,0:T(8,128)(2,1)} all-gather(bf16[96,192]{1,0:T(8,128)(2,1)S(1)} %copy-done.56), channel_id=1, replica_groups=mesh['fsdp'=8,'tp'=4] {'fsdp'}, dimensions={0}, use_global_device_ids=true | all-gather | bytes 331776 | tf_op jit(solution)/shard_map/all_gather | solution.py:175
  205.3 92.3 %while.50 = (s32[]{:T(128)}, bf16[4,512,3,64]{1,3,2,0:T(8,128)(2,1)}, f32[4,3,512,1]{2,1,3,0:T(4,128)}, s32[4,512]{1,0:T(4,128)S(1)}, s32[2048]{0:T(1024)S(1)}, ...) while((s32[]{:T(128)}, ...), condition=%wide.region_10.11_spmd.clone.clone, body=%wide.region_7.10_spmd.clone.sunk.clone | while | flops 842011136 | bytes 50469040 | solution.py:82
  304.1 36.6 %reduce-scatter.13.cloned.1.call-done = bf16[1,512,768]{2,1,0:T(8,128)(2,1)} async-done(((bf16[1,2048,768]{2,1,0:T(8,128)(2,1)}), bf16[1,512,768]{2,1,0:T(8,128)(2,1)}) %reduce-scatter.13.cloned.1.call-update) | async-done | bytes 786448 | tf_op jit(solution)/shard_map/reduce_scatter | solution.py:47
  349.9 27.1 %all-gather.9.cloned.1.call-done = bf16[1,2048,768]{2,1,0:T(8,128)(2,1)} async-done(((bf16[1,512,768]{2,1,0:T(8,128)(2,1)}), bf16[1,2048,768]{2,1,0:T(8,128)(2,1)}) %all-gather.9.cloned.1.call-update) | async-done | bytes 3145744 | tf_op jit(solution)/shard_map/all_gather | solution.py:39
  377.0 18.6 %fusion.47 = (bf16[2048,768]{1,0:T(8,128)(2,1)}, f32[2048,768]{1,0:T(8,128)}) fusion(bf16[768,768]{1,0:T(8,128)(2,1)} %all-gather.11.cloned.1.call-done, bf16[1,2048,768]{2,1,0:T(8,128)(2,1)} %all-gather.9.cloned.1.call-done), kind=kOutput, calls=%fused_computation.61 | convolution fusion | flops 2518155264 | bytes 13762560 | tf_op jit(solution)/shard_map/dot_general | solution.py:205
  395.6 25.2 %all-gather.13.cloned.1.call-done = bf16[768,768]{0,1:T(8,128)(2,1)} async-done(((bf16[768,96]{0,1:T(8,128)(2,1)}), bf16[768,768]{0,1:T(8,128)(2,1)}) %all-gather.13.cloned.1.call-update) | async-done | bytes 1179664 | tf_op jit(solution)/shard_map/all_gather | solution.py:203
  420.9 29.1 %all-gather.15.cloned.1.call-done = bf16[1,2048,768]{2,1,0:T(8,128)(2,1)} async-done(((bf16[1,512,768]{2,1,0:T(8,128)(2,1)}), bf16[1,2048,768]{2,1,0:T(8,128)(2,1)}) %all-gather.15.cloned.1.call-update) | async-done | bytes 3145744 | tf_op jit(solution)/shard_map/all_gather | solution.py:43
  469.0 31.4 %reduce-scatter.17.cloned.1.call-done = bf16[1,512,768]{2,1,0:T(8,128)(2,1)} async-done(((bf16[1,2048,768]{2,1,0:T(8,128)(2,1)}), bf16[1,512,768]{2,1,0:T(8,128)(2,1)}) %reduce-scatter.17.cloned.1.call-update) | async-done | bytes 786448 | tf_op jit(solution)/shard_map/reduce_scatter | solution.py:53
  500.5 40.4 %reduce-scatter.15.cloned.1.call-done = bf16[1,512,768]{2,1,0:T(8,128)(2,1)} async-done(((bf16[1,2048,768]{2,1,0:T(8,128)(2,1)}), bf16[1,512,768]{2,1,0:T(8,128)(2,1)}) %reduce-scatter.15.cloned.1.call-update) | async-done | bytes 786448 | tf_op jit(solution)/shard_map/reduce_scatter | solution.py:47
  547.6 28.4 %all-gather.17.cloned.1.call-done = bf16[1,2048,768]{2,1,0:T(8,128)(2,1)} async-done(((bf16[1,512,768]{2,1,0:T(8,128)(2,1)}), bf16[1,2048,768]{2,1,0:T(8,128)(2,1)}) %all-gather.17.cloned.1.call-update) | async-done | bytes 3145744 | tf_op jit(solution)/shard_map/all_gather | solution.py:43
  579.9 132.6 %while.51 = (s32[]{:T(128)}, f32[2048,3,64]{0,2,1:T(8,128)}, f32[2048,3,64]{0,2,1:T(8,128)}, f32[4,512,3,64]{1,3,2,0:T(8,128)}, bf16[4,512,3,64]{1,3,2,0:T(8,128...) while((s32[]{:T(128)}, f32[2048,3,64]{0,2,1:T(8,128)}, ...), condition=%wide.region_20.21_spmd.clone.clone, body=%wide.region_18.20_spmd.clone.sunk.clone | while | flops 2064617984 | bytes 169277904 | solution.py:116
  738.3 7.1 fusion.65
  760.5 23.0 %reduce-scatter.31.cloned.1.call-done = f32[96,192]{1,0:T(8,128)} async-done(((f32[768,192]{1,0:T(8,128)}), f32[96,192]{1,0:T(8,128)}) %reduce-scatter.31.cloned.1.call-update) | async-done | bytes 73744
  785.1 37.7 %reduce-scatter.19.cloned.1.call-done = bf16[1,512,768]{2,1,0:T(8,128)(2,1)} async-done(((bf16[1,2048,768]{2,1,0:T(8,128)(2,1)}), bf16[1,512,768]{2,1,0:T(8,128)(2,1)}) %reduce-scatter.19.cloned.1.call-update) | async-done | bytes 786448 | tf_op jit(solution)/shard_map/reduce_scatter | solution.py:53
  824.8 41.4 %all-reduce.12 = (f32[768]{0:T(1024)S(1)}, f32[768]{0:T(1024)S(1)}, f32[768]{0:T(1024)S(1)}, f32[768]{0:T(1024)S(1)}, f32[768]{0:T(1024)S(1)}, /*index=5*/f32[768]{0:T(1024)S(1)}, f32[4]{0:T(128)S(1)}, f32[]{:T(128)}) all-reduce(f32[768]{0:T(1024)S(1)} %get-tuple-element.306, ...), channel_id=12, replica_groups=mesh['fsdp'=8,'tp'=4] {'fsdp','tp'}, use_global_device_ids=true, to_apply=%region_35.36.clone | all-reduce | flops 4613 | bytes 36904
  873.7 23.4 %reduce-scatter.27.cloned.1.call-done = f32[96,768]{1,0:T(8,128)} async-done(((f32[768,768]{1,0:T(8,128)}), f32[96,768]{1,0:T(8,128)}) %reduce-scatter.27.cloned.1.call-update) | async-done | bytes 294928 | tf_op jit(solution)/shard_map/reduce_scatter | solution.py:242
  897.1 72.5 %reduce-scatter.29.cloned.1.call-done = f32[768,96]{0,1:T(8,128)} async-done(((f32[768,768]{0,1:T(8,128)}), f32[768,96]{0,1:T(8,128)}) %reduce-scatter.29.cloned.1.call-update) | async-done | bytes 294928 | tf_op jit(solution)/shard_map/reduce_scatter | solution.py:243
  969.5 65.8 %reduce-scatter.23.cloned.1.call-done = f32[96,192]{1,0:T(8,128)} async-done(((f32[768,192]{1,0:T(8,128)}), f32[96,192]{1,0:T(8,128)}) %reduce-scatter.23.cloned.1.call-update) | async-done | bytes 73744 | tf_op jit(solution)/shard_map/reduce_scatter | solution.py:296
  1035.4 65.4 %reduce-scatter.25.cloned.1.call-done = f32[96,192]{1,0:T(8,128)} async-done(((f32[768,192]{1,0:T(8,128)}), f32[96,192]{1,0:T(8,128)}) %reduce-scatter.25.cloned.1.call-update) | async-done | bytes 73744 | tf_op jit(solution)/shard_map/reduce_scatter | solution.py:297
  1100.7 65.8 %reduce-scatter.21.cloned.1.call-done = f32[96,192]{1,0:T(8,128)} async-done(((f32[768,192]{1,0:T(8,128)}), f32[96,192]{1,0:T(8,128)}) %reduce-scatter.21.cloned.1.call-update) | async-done | bytes 73744 | tf_op jit(solution)/shard_map/reduce_scatter | solution.py:295
  (434 shorter events, 347.5 us)
Async XLA Ops:
  8.1 148.7 %copy-start.56 = (bf16[96,192]{1,0:T(8,128)(2,1)S(1)}, bf16[96,192]{1,0:T(8,128)(2,1)}, u32[]{:S(2)}) copy-start(bf16[96,192]{1,0:T(8,128)(2,1)} %param.25) | copy-start | bytes 110596
  8.1 182.6 %all-gather.7.cloned.1.call-start = ((), (), s32[]{:S(2)}) async-start(), calls=%async_computation.10 | async-start | bytes 3932160 | tf_op jit(solution)/shard_map/all_gather | solution.py:39
  11.0 182.8 %copy-start.64 = (f32[512]{0:T(512)}, f32[512]{0:T(512)S(1)}, u32[]{:S(2)}) copy-start(f32[512]{0:T(512)S(1)} %add_rsqrt_fusion.3) | copy-start | bytes 6148
  58.4 135.4 %copy-start.58 = (f32[768]{0:T(1024)}, f32[768]{0:T(1024)S(1)}, u32[]{:S(2)}) copy-start(f32[768]{0:T(1024)S(1)} %get-tuple-element.372) | copy-start | bytes 9220
  60.8 279.9 %reduce-scatter.13.cloned.1.call-start = ((), (), s32[]{:S(2)}) async-start(), calls=%async_computation.11 | async-start | bytes 3932160 | tf_op jit(solution)/shard_map/reduce_scatter | solution.py:47
  61.7 138.2 %copy-start.62 = (f32[3,64]{1,0:T(4,128)}, f32[3,64]{1,0:T(4,128)S(1)}, u32[]{:S(2)}) copy-start(f32[3,64]{1,0:T(4,128)S(1)} %mul.406) | copy-start | bytes 2308
  62.1 138.2 %copy-start.68 = (f32[3,64]{1,0:T(4,128)}, f32[3,64]{1,0:T(4,128)S(1)}, u32[]{:S(2)}) copy-start(f32[3,64]{1,0:T(4,128)S(1)} %mul.400) | copy-start | bytes 2308
  302.2 47.7 %all-gather.11.cloned.1.call-start = ((), (), s32[]{:S(2)}) async-start(), calls=%async_computation.13 | async-start | bytes 1327104 | tf_op jit(solution)/shard_map/all_gather | solution.py:202
  302.8 74.2 %all-gather.9.cloned.1.call-start = ((), (), s32[]{:S(2)}) async-start(), calls=%async_computation.12 | async-start | bytes 3932160 | tf_op jit(solution)/shard_map/all_gather | solution.py:39
  348.5 72.3 %all-gather.13.cloned.1.call-start = ((), (), s32[]{:S(2)}) async-start(), calls=%async_computation.14 | async-start | bytes 1327104 | tf_op jit(solution)/shard_map/all_gather | solution.py:203
  349.1 100.9 %all-gather.15.cloned.1.call-start = ((), (), s32[]{:S(2)}) async-start(), calls=%async_computation.16 | async-start | bytes 3932160 | tf_op jit(solution)/shard_map/all_gather | solution.py:43
  349.8 150.6 %reduce-scatter.17.cloned.1.call-start = ((), (), s32[]{:S(2)}) async-start(), calls=%async_computation.17 | async-start | bytes 3932160 | tf_op jit(solution)/shard_map/reduce_scatter | solution.py:53
  462.4 78.5 %reduce-scatter.15.cloned.1.call-start = ((), (), s32[]{:S(2)}) async-start(), calls=%async_computation.15 | async-start | bytes 3932160 | tf_op jit(solution)/shard_map/reduce_scatter | solution.py:47
  469.0 107.0 %all-gather.17.cloned.1.call-start = ((), (), s32[]{:S(2)}) async-start(), calls=%async_computation.18 | async-start | bytes 3932160 | tf_op jit(solution)/shard_map/all_gather | solution.py:43
  547.5 235.9 %reduce-scatter.31.cloned.1.call-start = ((), (), s32[]{:S(2)}) async-start(), calls=%async_computation.25 | async-start | bytes 884736
  579.8 132.7 %copy-start.41 = (f32[2048,3]{0,1:T(4,128)S(1)}, f32[2048,3]{0,1:T(4,128)}, u32[]{:S(2)}) copy-start(f32[2048,3]{0,1:T(4,128)} %copy-done.40) | copy-start | bytes 73732
  579.9 132.7 %copy-start.45 = (f32[2048,3]{0,1:T(4,128)S(1)}, f32[2048,3]{0,1:T(4,128)}, u32[]{:S(2)}) copy-start(f32[2048,3]{0,1:T(4,128)} %copy-done.44) | copy-start | bytes 73732
  579.9 132.7 %copy-start.69 = (f32[3,64]{1,0:T(4,128)S(1)}, f32[3,64]{1,0:T(4,128)}, u32[]{:S(2)}) copy-start(f32[3,64]{1,0:T(4,128)} %copy-done.68) | copy-start | bytes 2308
  720.8 101.9 %reduce-scatter.19.cloned.1.call-start = ((), (), s32[]{:S(2)}) async-start(), calls=%async_computation.19 | async-start | bytes 3932160 | tf_op jit(solution)/shard_map/reduce_scatter | solution.py:53
  730.0 167.0 %reduce-scatter.27.cloned.1.call-start = ((), (), s32[]{:S(2)}) async-start(), calls=%async_computation.23 | async-start | bytes 2654208 | tf_op jit(solution)/shard_map/reduce_scatter | solution.py:242
  738.0 231.6 %reduce-scatter.29.cloned.1.call-start = ((), (), s32[]{:S(2)}) async-start(), calls=%async_computation.24 | async-start | bytes 2654208 | tf_op jit(solution)/shard_map/reduce_scatter | solution.py:243
  745.4 289.9 %reduce-scatter.23.cloned.1.call-start = ((), (), s32[]{:S(2)}) async-start(), calls=%async_computation.21 | async-start | bytes 884736 | tf_op jit(solution)/shard_map/reduce_scatter | solution.py:296
  748.6 352.1 %reduce-scatter.25.cloned.1.call-start = ((), (), s32[]{:S(2)}) async-start(), calls=%async_computation.22 | async-start | bytes 884736 | tf_op jit(solution)/shard_map/reduce_scatter | solution.py:297
  751.7 414.8 %reduce-scatter.21.cloned.1.call-start = ((), (), s32[]{:S(2)}) async-start(), calls=%async_computation.20 | async-start | bytes 884736 | tf_op jit(solution)/shard_map/reduce_scatter | solution.py:295
  (107 other events, 1461.1 us)
Sparse Core Ops, SparseCore 0:
  60.9 28.6 all-gather.6
  302.3 38.2 reduce-scatter.12
  462.5 37.9 reduce-scatter.16
  502.9 37.9 reduce-scatter.14
Sparse Core Ops, SparseCore 1:
  305.1 41.8 all-gather.10
  348.6 28.3 all-gather.8
  379.3 41.5 all-gather.12
  423.1 26.8 all-gather.14
  547.6 28.3 all-gather.16
  720.9 62.5 reduce-scatter.30
  785.9 36.9 reduce-scatter.18
  827.1 69.9 reduce-scatter.26
  901.4 68.1 reduce-scatter.28
  973.8 61.5 reduce-scatter.22
  1039.1 61.6 reduce-scatter.24
  1105.0 61.5 reduce-scatter.20
where the time goes:
time: 1180 us; the launch traced here: 1170 us
  waiting for transfers between devices  574 us (49%)
  matrix products  225 us (19%)
  blocking collectives  210 us (18%)
  other arithmetic  103 us (9%)
  local copies, waits for them, and re-layouts  42 us (4%)
  between operations  17.5 us (1%)
    unnamed x2, blocking collectives  83.7 us
    reduce_scatter x2, waiting for transfers between devices, reduce_tokens(): lax.psum_scatter(values.astype(jnp.bfloat16), 'tp', scatter_dimension=1,...  77 us
    reduce_scatter x1, waiting for transfers between devices, local(): lax.psum_scatter(grad_down, 'fsdp', scatter_dimension=1, tiled=True)  72.5 us
    reduce_scatter x2, waiting for transfers between devices, reduce_grads(): lax.psum_scatter(values.astype(jnp.bfloat16), 'tp', scatter_dimension=1,...  69.1 us
    reduce_scatter x1, waiting for transfers between devices, local(): lax.psum_scatter(grad_wkey, 'fsdp', scatter_dimension=0, tiled=True)  65.8 us
    reduce_scatter x1, waiting for transfers between devices, local(): lax.psum_scatter(grad_wquery, 'fsdp', scatter_dimension=0, tiled=True)  65.8 us
    reduce_scatter x1, waiting for transfers between devices, local(): lax.psum_scatter(grad_wvalue, 'fsdp', scatter_dimension=0, tiled=True)  65.4 us
    all_gather x2, waiting for transfers between devices, gather_grads(): return lax.all_gather(values, 'tp', axis=1, tiled=True)  57.5 us
  transfers between devices with their start and end apart: 16, of which 14 were waited for; matrix products, arithmetic and copies ran while one was open for 7% of the time, Pallas kernels for 0%

commit v1 on v0

--- a/solution.py
+++ b/solution.py
@@ -169,11 +169,40 @@
     kgain_here = lax.dynamic_slice_in_dim(gain_key, tp_place * local_width, local_width, 0).reshape(
         heads_local, HD
     )
+
+    def answer_shards(panel, axis_id):
+        mid_arr, block_last, current_value = (
+            lax.axis_size(axis_id),
+            lax.axis_index(axis_id),
+            panel.shape[1],
+        )
+        slots = [ii * mid_arr if nth == 1 else ii for nth, ii in enumerate(panel.shape)]
+        o_now = jnp.zeros(slots, panel.dtype)
+        inter = lax.dynamic_update_slice_in_dim(o_now, panel, block_last * current_value, axis=1)
+        w2 = top = panel
+        for k0 in range(1, mid_arr // 2 + 1):
+            w2 = lax.ppermute(
+                w2, axis_name=axis_id, perm=[(nth, (nth + 1) % mid_arr) for nth in range(mid_arr)]
+            )
+            inter = lax.dynamic_update_slice_in_dim(
+                inter, w2, (block_last - k0) % mid_arr * current_value, axis=1
+            )
+            if 2 * k0 < mid_arr:
+                top = lax.ppermute(
+                    top,
+                    axis_name=axis_id,
+                    perm=[(nth, (nth - 1) % mid_arr) for nth in range(mid_arr)],
+                )
+                inter = lax.dynamic_update_slice_in_dim(
+                    inter, top, (block_last + k0) % mid_arr * current_value, axis=1
+                )
+        return inter
+
     front_query, front_key, front_value, front_out = (
         lax.all_gather(w_query, "fsdp", axis=0, tiled=True),
         lax.all_gather(w_key, "fsdp", axis=0, tiled=True),
         lax.all_gather(w_value, "fsdp", axis=0, tiled=True),
-        lax.all_gather(w_out, "fsdp", axis=1, tiled=True),
+        answer_shards(w_out, "fsdp"),
     )
     inputs = tokens.astype(jnp.float32)
     hidden, normed_one, inverse_one = normalise(inputs, gain_one, shift_one)

time: 1180 us -> 1170 us (level)
  waiting for transfers between devices: 574 us -> 549 us
  starting transfers between devices: 0.94 us -> 15.2 us
    all_gather x2, waiting for transfers between devices: 57.5 us -> 29.1 us  [gather_grads(): return lax.all_gather(values, 'tp', axis=1, tiled=True)]
    ppermute x0 -> x7, starting transfers between devices: none -> 14.2 us  [the longest x3 11.9 us: answer_shards(): lax.ppermute(top, axis_name=axis_id, perm=[(nth, (nth - 1) % mid_arr) for...]
  transfers between devices with their start and end apart: 16 -> 23, of which waited for: 14 -> 14; matrix products, arithmetic and copies ran while one was open for 7% -> 7% of each run, Pallas kernels for 0% -> 0%
where the time goes in v1:
time: 1170 us; the launch traced here: 1160 us
  waiting for transfers between devices  549 us (47%)
  matrix products  225 us (19%)
  blocking collectives  209 us (18%)
  other arithmetic  103 us (9%)
  local copies, waits for them, and re-layouts  44.9 us (4%)
  between operations  17.6 us (2%)
  starting transfers between devices  15.2 us (1%)
    unnamed x2, blocking collectives  84.1 us
    reduce_scatter x2, waiting for transfers between devices, reduce_tokens(): lax.psum_scatter(values.astype(jnp.bfloat16), 'tp', scatter_dimension=1,...  79.6 us
    reduce_scatter x1, waiting for transfers between devices, local(): lax.psum_scatter(grad_down, 'fsdp', scatter_dimension=1, tiled=True)  72.5 us
    reduce_scatter x2, waiting for transfers between devices, reduce_grads(): lax.psum_scatter(values.astype(jnp.bfloat16), 'tp', scatter_dimension=1,...  69.1 us
    reduce_scatter x1, waiting for transfers between devices, local(): lax.psum_scatter(grad_wkey, 'fsdp', scatter_dimension=0, tiled=True)  65.9 us
    reduce_scatter x1, waiting for transfers between devices, local(): lax.psum_scatter(grad_wquery, 'fsdp', scatter_dimension=0, tiled=True)  65.8 us
    reduce_scatter x1, waiting for transfers between devices, local(): lax.psum_scatter(grad_wvalue, 'fsdp', scatter_dimension=0, tiled=True)  65.4 us
    dot_general x8, matrix products, block_scores(): jnp.einsum('qhd,khd->hqk', query, keyed, preferred_element_type=jnp.float32)  38.9 us
  transfers between devices with their start and end apart: 23, of which 14 were waited for; matrix products, arithmetic and copies ran while one was open for 7% of the time, Pallas kernels for 0%

profile of v1, /device:TPU:0, one launch (start us, length us, event | category | flops | bytes accessed | tf_op | source)
XLA Modules:
  0.0 1164.5 jit_solution(11157167689089633207)
XLA Ops:
  16.0 42.4 %all-reduce.13 = (f32[768]{0:T(1024)}, f32[768]{0:T(1024)}, f32[768]{0:T(1024)S(1)}, f32[768]{0:T(1024)S(1)}, f32[768]{0:T(1024)S(1)}, /*index=5*/f32[768]{0:T(1024)S(1)}) all-reduce(f32[768]{0:T(1024)S(1)} %dynamic-update-slice.5, f32[768]{0:T(1024)S(1)} %dynamic-update-slice.4, ...), channel_id=1, replica_groups=mesh['fsdp'=8,'tp'=4] {'fsdp','tp'}, use_global_device_ids=true, to_apply=%add.5 | all-reduce | flops 4608 | bytes 36864
  67.8 31.1 %all_gather.56 = bf16[768,192]{1,0:T(8,128)(2,1)S(1)} all-gather(bf16[96,192]{1,0:T(8,128)(2,1)S(1)} %copy-done.54), channel_id=1, replica_groups=mesh['fsdp'=8,'tp'=4] {'fsdp'}, dimensions={0}, use_global_device_ids=true | all-gather | bytes 331776 | tf_op jit(solution)/shard_map/all_gather | solution.py:202
  103.7 31.1 %all_gather.58 = bf16[768,192]{1,0:T(8,128)(2,1)S(1)} all-gather(bf16[96,192]{1,0:T(8,128)(2,1)S(1)} %copy-done.55), channel_id=1, replica_groups=mesh['fsdp'=8,'tp'=4] {'fsdp'}, dimensions={0}, use_global_device_ids=true | all-gather | bytes 331776 | tf_op jit(solution)/shard_map/all_gather | solution.py:203
  139.5 31.5 %all_gather.60 = bf16[768,192]{1,0:T(8,128)(2,1)S(1)} all-gather(bf16[96,192]{1,0:T(8,128)(2,1)S(1)} %copy-done.56), channel_id=1, replica_groups=mesh['fsdp'=8,'tp'=4] {'fsdp'}, dimensions={0}, use_global_device_ids=true | all-gather | bytes 331776 | tf_op jit(solution)/shard_map/all_gather | solution.py:204
  191.6 91.9 %while.50 = (s32[]{:T(128)}, bf16[4,512,3,64]{1,3,2,0:T(8,128)(2,1)}, f32[4,3,512,1]{2,1,3,0:T(4,128)}, s32[4,512]{1,0:T(4,128)S(1)}, s32[2048]{0:T(1024)S(1)}, ...) while((s32[]{:T(128)}, ...), condition=%wide.region_10.11_spmd.clone.clone, body=%wide.region_7.10_spmd.clone.sunk.clone | while | flops 842011136 | bytes 50469040 | solution.py:82
  200.0 6.8 exponential_reduce_fusion.3
  289.5 39.2 %reduce-scatter.13.cloned.1.call-done = bf16[1,512,768]{2,1,0:T(8,128)(2,1)} async-done(((bf16[1,2048,768]{2,1,0:T(8,128)(2,1)}), bf16[1,512,768]{2,1,0:T(8,128)(2,1)}) %reduce-scatter.13.cloned.1.call-update) | async-done | bytes 786448 | tf_op jit(solution)/shard_map/reduce_scatter | solution.py:47
  337.3 27.1 %all-gather.9.cloned.1.call-done = bf16[1,2048,768]{2,1,0:T(8,128)(2,1)} async-done(((bf16[1,512,768]{2,1,0:T(8,128)(2,1)}), bf16[1,2048,768]{2,1,0:T(8,128)(2,1)}) %all-gather.9.cloned.1.call-update) | async-done | bytes 3145744 | tf_op jit(solution)/shard_map/all_gather | solution.py:39
  364.4 18.5 %fusion.47 = (bf16[2048,768]{1,0:T(8,128)(2,1)}, f32[2048,768]{1,0:T(8,128)}) fusion(bf16[768,768]{1,0:T(8,128)(2,1)} %all-gather.11.cloned.1.call-done, bf16[1,2048,768]{2,1,0:T(8,128)(2,1)} %all-gather.9.cloned.1.call-done), kind=kOutput, calls=%fused_computation.61 | convolution fusion | flops 2518155264 | bytes 13762560 | tf_op jit(solution)/shard_map/dot_general | solution.py:234
  383.0 25.3 %all-gather.13.cloned.1.call-done = bf16[768,768]{0,1:T(8,128)(2,1)} async-done(((bf16[768,96]{0,1:T(8,128)(2,1)}), bf16[768,768]{0,1:T(8,128)(2,1)}) %all-gather.13.cloned.1.call-update) | async-done | bytes 1179664 | tf_op jit(solution)/shard_map/all_gather | solution.py:232
  408.3 29.1 %all-gather.15.cloned.1.call-done = bf16[1,2048,768]{2,1,0:T(8,128)(2,1)} async-done(((bf16[1,512,768]{2,1,0:T(8,128)(2,1)}), bf16[1,2048,768]{2,1,0:T(8,128)(2,1)}) %all-gather.15.cloned.1.call-update) | async-done | bytes 3145744 | tf_op jit(solution)/shard_map/all_gather | solution.py:43
  456.4 31.4 %reduce-scatter.17.cloned.1.call-done = bf16[1,512,768]{2,1,0:T(8,128)(2,1)} async-done(((bf16[1,2048,768]{2,1,0:T(8,128)(2,1)}), bf16[1,512,768]{2,1,0:T(8,128)(2,1)}) %reduce-scatter.17.cloned.1.call-update) | async-done | bytes 786448 | tf_op jit(solution)/shard_map/reduce_scatter | solution.py:53
  487.9 40.4 %reduce-scatter.15.cloned.1.call-done = bf16[1,512,768]{2,1,0:T(8,128)(2,1)} async-done(((bf16[1,2048,768]{2,1,0:T(8,128)(2,1)}), bf16[1,512,768]{2,1,0:T(8,128)(2,1)}) %reduce-scatter.15.cloned.1.call-update) | async-done | bytes 786448 | tf_op jit(solution)/shard_map/reduce_scatter | solution.py:47
  535.1 31.2 %all_gather.68 = bf16[192,768]{0,1:T(8,128)(2,1)S(1)} all-gather(bf16[192,96]{0,1:T(8,128)(2,1)S(1)} %copy.45), channel_id=1, replica_groups=mesh['fsdp'=8,'tp'=4] {'fsdp'}, dimensions={1}, use_global_device_ids=true | all-gather | bytes 331776 | tf_op jit(solution)/shard_map/all_gather | solution.py:257
  570.1 132.6 %while.51 = (s32[]{:T(128)}, f32[2048,3,64]{0,2,1:T(8,128)}, f32[2048,3,64]{0,2,1:T(8,128)}, f32[4,512,3,64]{1,3,2,0:T(8,128)}, bf16[4,512,3,64]{1,3,2,0:T(8,128...) while((s32[]{:T(128)}, f32[2048,3,64]{0,2,1:T(8,128)}, ...), condition=%wide.region_20.21_spmd.clone.clone, body=%wide.region_18.20_spmd.clone.sunk.clone | while | flops 2064617984 | bytes 169277904 | solution.py:116
  728.5 7.1 fusion.65
  750.6 23.0 %reduce-scatter.31.cloned.1.call-done = f32[96,192]{1,0:T(8,128)} async-done(((f32[768,192]{1,0:T(8,128)}), f32[96,192]{1,0:T(8,128)}) %reduce-scatter.31.cloned.1.call-update) | async-done | bytes 73744
  775.3 37.7 %reduce-scatter.19.cloned.1.call-done = bf16[1,512,768]{2,1,0:T(8,128)(2,1)} async-done(((bf16[1,2048,768]{2,1,0:T(8,128)(2,1)}), bf16[1,512,768]{2,1,0:T(8,128)(2,1)}) %reduce-scatter.19.cloned.1.call-update) | async-done | bytes 786448 | tf_op jit(solution)/shard_map/reduce_scatter | solution.py:53
  814.9 41.7 %all-reduce.12 = (f32[768]{0:T(1024)S(1)}, f32[768]{0:T(1024)S(1)}, f32[768]{0:T(1024)S(1)}, f32[768]{0:T(1024)S(1)}, f32[768]{0:T(1024)S(1)}, /*index=5*/f32[768]{0:T(1024)S(1)}, f32[4]{0:T(128)S(1)}, f32[]{:T(128)}) all-reduce(f32[768]{0:T(1024)S(1)} %get-tuple-element.306, ...), channel_id=12, replica_groups=mesh['fsdp'=8,'tp'=4] {'fsdp','tp'}, use_global_device_ids=true, to_apply=%region_35.36.clone | all-reduce | flops 4613 | bytes 36904
  864.2 23.0 %reduce-scatter.27.cloned.1.call-done = f32[96,768]{1,0:T(8,128)} async-done(((f32[768,768]{1,0:T(8,128)}), f32[96,768]{1,0:T(8,128)}) %reduce-scatter.27.cloned.1.call-update) | async-done | bytes 294928 | tf_op jit(solution)/shard_map/reduce_scatter | solution.py:271
  887.2 72.5 %reduce-scatter.29.cloned.1.call-done = f32[768,96]{0,1:T(8,128)} async-done(((f32[768,768]{0,1:T(8,128)}), f32[768,96]{0,1:T(8,128)}) %reduce-scatter.29.cloned.1.call-update) | async-done | bytes 294928 | tf_op jit(solution)/shard_map/reduce_scatter | solution.py:272
  959.7 65.9 %reduce-scatter.23.cloned.1.call-done = f32[96,192]{1,0:T(8,128)} async-done(((f32[768,192]{1,0:T(8,128)}), f32[96,192]{1,0:T(8,128)}) %reduce-scatter.23.cloned.1.call-update) | async-done | bytes 73744 | tf_op jit(solution)/shard_map/reduce_scatter | solution.py:325
  1025.7 65.4 %reduce-scatter.25.cloned.1.call-done = f32[96,192]{1,0:T(8,128)} async-done(((f32[768,192]{1,0:T(8,128)}), f32[96,192]{1,0:T(8,128)}) %reduce-scatter.25.cloned.1.call-update) | async-done | bytes 73744 | tf_op jit(solution)/shard_map/reduce_scatter | solution.py:326
  1091.1 65.8 %reduce-scatter.21.cloned.1.call-done = f32[96,192]{1,0:T(8,128)} async-done(((f32[768,192]{1,0:T(8,128)}), f32[96,192]{1,0:T(8,128)}) %reduce-scatter.21.cloned.1.call-update) | async-done | bytes 73744 | tf_op jit(solution)/shard_map/reduce_scatter | solution.py:324
  (449 shorter events, 358.1 us)
Async XLA Ops:
  8.1 169.0 %all-gather.7.cloned.1.call-start = ((), (), s32[]{:S(2)}) async-start(), calls=%async_computation.10 | async-start | bytes 3932160 | tf_op jit(solution)/shard_map/all_gather | solution.py:39
  9.5 165.6 %copy-start.52 = (f32[512]{0:T(512)}, f32[512]{0:T(512)S(1)}, u32[]{:S(2)}) copy-start(f32[512]{0:T(512)S(1)} %broadcast_multiply_fusion.11) | copy-start | bytes 6148
  60.8 267.9 %reduce-scatter.13.cloned.1.call-start = ((), (), s32[]{:S(2)}) async-start(), calls=%async_computation.11 | async-start | bytes 3932160 | tf_op jit(solution)/shard_map/reduce_scatter | solution.py:47
  60.8 6.9 collective-permute-start
  63.2 35.7 %collective-permute-start.1 = (bf16[192,96]{1,0:T(8,128)(2,1)S(1)}, bf16[192,96]{1,0:T(8,128)(2,1)S(1)}, u32[]{:S(2)}, u32[]{:S(2)}) collective-permute-start(bf16[192,96]{1,0:T(8,128)(2,1)S(1)} %copy-done.50), channel_id=1, source_target_pairs={{0,28},{4,0},{8,4},{12,8},{16,12},{20,16},{24,20},{28,24},{1,29},{... | collective-permute-start | bytes 110600 | tf_op jit(solution)/shard_map/ppermute | solution.py:191
  67.8 35.9 %collective-permute-start.2 = (bf16[192,96]{1,0:T(8,128)(2,1)S(1)}, bf16[192,96]{1,0:T(8,128)(2,1)S(1)}, u32[]{:S(2)}, u32[]{:S(2)}) collective-permute-start(bf16[192,96]{1,0:T(8,128)(2,1)S(1)} %collective-permute-done), channel_id=1, source_target_pairs={{0,4},{4,8},{8,12},{12,16},{16,20},{20,24},{24,28},{28,0},{1,5},{5... | collective-permute-start | bytes 110600 | tf_op jit(solution)/shard_map/ppermute | solution.py:184
  98.9 35.9 %collective-permute-start.3 = (bf16[192,96]{1,0:T(8,128)(2,1)S(1)}, bf16[192,96]{1,0:T(8,128)(2,1)S(1)}, u32[]{:S(2)}, u32[]{:S(2)}) collective-permute-start(bf16[192,96]{1,0:T(8,128)(2,1)S(1)} %collective-permute-done.1), channel_id=1, source_target_pairs={{0,28},{4,0},{8,4},{12,8},{16,12},{20,16},{24,20},{28,24},{1,29},{... | collective-permute-start | bytes 110600 | tf_op jit(solution)/shard_map/ppermute | solution.py:191
  103.7 35.8 %collective-permute-start.4 = (bf16[192,96]{1,0:T(8,128)(2,1)S(1)}, bf16[192,96]{1,0:T(8,128)(2,1)S(1)}, u32[]{:S(2)}, u32[]{:S(2)}) collective-permute-start(bf16[192,96]{1,0:T(8,128)(2,1)S(1)} %collective-permute-done.2), channel_id=1, source_target_pairs={{0,4},{4,8},{8,12},{12,16},{16,20},{20,24},{24,28},{28,0},{1,5},{5... | collective-permute-start | bytes 110600 | tf_op jit(solution)/shard_map/ppermute | solution.py:184
  134.8 41.4 %collective-permute-start.5 = (bf16[192,96]{1,0:T(8,128)(2,1)S(1)}, bf16[192,96]{1,0:T(8,128)(2,1)S(1)}, u32[]{:S(2)}, u32[]{:S(2)}) collective-permute-start(bf16[192,96]{1,0:T(8,128)(2,1)S(1)} %collective-permute-done.3), channel_id=1, source_target_pairs={{0,28},{4,0},{8,4},{12,8},{16,12},{20,16},{24,20},{28,24},{1,29},{... | collective-permute-start | bytes 110600 | tf_op jit(solution)/shard_map/ppermute | solution.py:191
  139.5 37.3 %collective-permute-start.6 = (bf16[192,96]{1,0:T(8,128)(2,1)S(1)}, bf16[192,96]{1,0:T(8,128)(2,1)S(1)}, u32[]{:S(2)}, u32[]{:S(2)}) collective-permute-start(bf16[192,96]{1,0:T(8,128)(2,1)S(1)} %collective-permute-done.4), channel_id=1, source_target_pairs={{0,4},{4,8},{8,12},{12,16},{16,20},{20,24},{24,28},{28,0},{1,5},{5... | collective-permute-start | bytes 110600 | tf_op jit(solution)/shard_map/ppermute | solution.py:184
  288.2 49.1 %all-gather.11.cloned.1.call-start = ((), (), s32[]{:S(2)}) async-start(), calls=%async_computation.13 | async-start | bytes 1327104 | tf_op jit(solution)/shard_map/all_gather | solution.py:231
  288.8 75.6 %all-gather.9.cloned.1.call-start = ((), (), s32[]{:S(2)}) async-start(), calls=%async_computation.12 | async-start | bytes 3932160 | tf_op jit(solution)/shard_map/all_gather | solution.py:39
  335.9 72.3 %all-gather.13.cloned.1.call-start = ((), (), s32[]{:S(2)}) async-start(), calls=%async_computation.14 | async-start | bytes 1327104 | tf_op jit(solution)/shard_map/all_gather | solution.py:232
  336.5 100.9 %all-gather.15.cloned.1.call-start = ((), (), s32[]{:S(2)}) async-start(), calls=%async_computation.16 | async-start | bytes 3932160 | tf_op jit(solution)/shard_map/all_gather | solution.py:43
  337.3 150.6 %reduce-scatter.17.cloned.1.call-start = ((), (), s32[]{:S(2)}) async-start(), calls=%async_computation.17 | async-start | bytes 3932160 | tf_op jit(solution)/shard_map/reduce_scatter | solution.py:53
  449.8 78.5 %reduce-scatter.15.cloned.1.call-start = ((), (), s32[]{:S(2)}) async-start(), calls=%async_computation.15 | async-start | bytes 3932160 | tf_op jit(solution)/shard_map/reduce_scatter | solution.py:47
  456.4 109.9 %all-gather.17.cloned.1.call-start = ((), (), s32[]{:S(2)}) async-start(), calls=%async_computation.18 | async-start | bytes 3932160 | tf_op jit(solution)/shard_map/all_gather | solution.py:43
  534.9 238.7 %reduce-scatter.31.cloned.1.call-start = ((), (), s32[]{:S(2)}) async-start(), calls=%async_computation.25 | async-start | bytes 884736
  711.1 101.9 %reduce-scatter.19.cloned.1.call-start = ((), (), s32[]{:S(2)}) async-start(), calls=%async_computation.19 | async-start | bytes 3932160 | tf_op jit(solution)/shard_map/reduce_scatter | solution.py:53
  720.2 167.0 %reduce-scatter.27.cloned.1.call-start = ((), (), s32[]{:S(2)}) async-start(), calls=%async_computation.23 | async-start | bytes 2654208 | tf_op jit(solution)/shard_map/reduce_scatter | solution.py:271
  728.2 231.6 %reduce-scatter.29.cloned.1.call-start = ((), (), s32[]{:S(2)}) async-start(), calls=%async_computation.24 | async-start | bytes 2654208 | tf_op jit(solution)/shard_map/reduce_scatter | solution.py:272
  735.6 290.1 %reduce-scatter.23.cloned.1.call-start = ((), (), s32[]{:S(2)}) async-start(), calls=%async_computation.21 | async-start | bytes 884736 | tf_op jit(solution)/shard_map/reduce_scatter | solution.py:325
  738.8 352.3 %reduce-scatter.25.cloned.1.call-start = ((), (), s32[]{:S(2)}) async-start(), calls=%async_computation.22 | async-start | bytes 884736 | tf_op jit(solution)/shard_map/reduce_scatter | solution.py:326
  741.9 415.0 %reduce-scatter.21.cloned.1.call-start = ((), (), s32[]{:S(2)}) async-start(), calls=%async_computation.20 | async-start | bytes 884736 | tf_op jit(solution)/shard_map/reduce_scatter | solution.py:324
  (110 other events, 2521.5 us)
Sparse Core Ops, SparseCore 0:
  60.9 28.6 all-gather.6
  288.3 40.3 reduce-scatter.12
  449.9 37.9 reduce-scatter.16
  490.3 37.9 reduce-scatter.14
Sparse Core Ops, SparseCore 1:
  291.1 43.8 all-gather.10
  336.5 27.8 all-gather.8
  366.7 41.5 all-gather.12
  410.5 26.8 all-gather.14
  535.0 28.3 all-gather.16
  711.1 62.4 reduce-scatter.30
  776.0 36.8 reduce-scatter.18
  817.3 69.9 reduce-scatter.26
  891.6 68.1 reduce-scatter.28
  964.0 61.6 reduce-scatter.22
  1029.4 61.6 reduce-scatter.24
  1095.3 61.5 reduce-scatter.20
